TPU v7x, 32 devices: a whole 2x2x4 slice. The times are simulated.
32 devices in a mesh: ens: 2 (over y), tm: 4 (over x, core), lat: 4 (over z).
Axes of the slice: x: 2, y: 2, z: 4, core: 2. Of those that a mesh axis runs over, the one named last changes fastest.
Arguments:
- departures: float32 [8, 8, 69, 256], P(('ens', 'tm'), 'lat'), parts along dimension 0, may hold values from -6 to 6
- error_precision: float32 [8, 8, 69, 256], P(('ens', 'tm'), 'lat'), parts along dimension 0, may hold values from 0.5 to 4
- trajectory: bfloat16 [8, 8, 69, 256], P(('ens', 'tm'), 'lat'), parts along dimension 0, may hold values from -6 to 6
- conv_in: bfloat16 [3, 3, 128, 69], replicated, may hold values from -0.25 to 0.25
- conv_out: bfloat16 [3, 3, 69, 128], replicated, may hold values from -0.1875 to 0.1875
- hidden_bias: float32 [128], replicated, may hold values from -1 to 1
- step_counts: int32 [8], P(('ens', 'tm')), parts along dimension 0, may hold values from 1 to 2, as said below
- obs_tiles: int32 [8, 1024], P(('ens', 'tm'), 'lat'), parts along dimension 0, may hold values from 0 to 275
- obs_weights: float32 [8, 1024, 128], P(('ens', 'tm'), 'lat'), parts along dimension 0, may hold values from -0.5 to 0.5
- innovations: float32 [8, 1024], P(('ens', 'tm'), 'lat'), parts along dimension 0, may hold values from -6 to 6
- obs_precision: float32 [8, 1024], P(('ens', 'tm'), 'lat'), parts along dimension 0, may hold values from 0.5 to 4
Outputs:
- increment: float32 [8, 8, 69, 256], P(('ens', 'tm'), 'lat'), parts along dimension 0
- residual: float32 [8, 8, 69, 256], P(('ens', 'tm'), 'lat'), parts along dimension 0
There are 2 independent parts, one for each index of `ens`. A program takes and returns all parts, laid end to end along the dimension named above; an argument that names none is the same for every part. Nothing has to cross between parts.
Inputs may be any that keep to these rules, and one draw needn't show every extreme that they name: sub-window k runs step_counts[k] of its 2 hourly steps; some sub-window runs all of them.
All inputs are finite; a program needn't handle non-finite values.
Results may differ from a plain program's by a relative error of at most 0.02.
Values may be sent and summed in bfloat16 or wider, within the bound.
No kernel may reach another device: no remote copies, remote signals or barrier semaphores. Data moves between devices by JAX's collectives and lax.ppermute only.
A program may use at most 64 MiB of HBM per device.

v0:
```python
import jax
import jax.numpy as jnp
from jax import lax
from jax.sharding import PartitionSpec as P

TILE = 128
STEPS = 2
ITERS = 2


def padded_2(cells, sides, width):
    for axis, dim in sides:
        count = lax.axis_size(axis)
        ends = count - 1
        head = lax.slice_in_dim(cells, 0, width, axis=dim)
        tail = lax.slice_in_dim(cells, cells.shape[dim] - width, cells.shape[dim], axis=dim)
        cells = jnp.concatenate(
            [
                lax.ppermute(tail, axis, [(i, (i + 1) % count) for i in range(ends)]),
                cells,
                lax.ppermute(head, axis, [((i + 1) % count, i) for i in range(ends)]),
            ],
            axis=dim,
        )
    return cells


def from_behind(value, axis, steps):
    count = lax.axis_size(axis)
    leading, last = (max(0, -steps), min(count, count - steps))
    return lax.ppermute(value, axis, [(source, source + steps) for source in range(leading, last)])


def convolve_padded(padded, kernel):
    out_rows = padded.shape[0] - 2
    lon_len = padded.shape[2]
    wrapped = jnp.concatenate([padded[:, :, -1:], padded, padded[:, :, :1]], axis=2)
    accumulated = None
    for row_off in range(3):
        for col_off in range(3):
            window = wrapped[row_off : row_off + out_rows, :, col_off : col_off + lon_len]
            term = jnp.einsum(
                "oi,ril->rol", kernel[row_off, col_off], window, preferred_element_type=jnp.float32
            )
            accumulated = term if accumulated is None else accumulated + term
    return accumulated


def flipped(kernel):
    return jnp.transpose(kernel[::-1, ::-1], (0, 1, 3, 2))


def rim_wide(source):
    return padded_2(source, (("lat", 0),), 2)


def shift_up(source):
    return from_behind(source.astype(jnp.bfloat16), "tm", -1).astype(source.dtype)


def global_squares(source):
    return lax.psum(jnp.sum(source * source), ("tm", "lat"))


def per_device(
    departures,
    error_precision,
    trajectory,
    conv_in,
    conv_out,
    hidden_bias,
    step_counts,
    obs_tiles,
    obs_weights,
    innovations,
    obs_precision,
):
    precision = error_precision[0]
    own_count = step_counts[0]
    tile_index = obs_tiles[0]
    weights = obs_weights[0]
    innovation = innovations[0]
    obs_scale = obs_precision[0]
    back_in = flipped(conv_in)
    back_out = flipped(conv_out)
    trajectory_ext = padded_2(trajectory[0], (("lat", 0),), 1)
    gate_factor = (
        1.0 - jnp.tanh(convolve_padded(trajectory_ext, conv_in) + hidden_bias[:, None]) ** 2
    ).astype(jnp.bfloat16)
    gate_wide = padded_2(gate_factor, (("lat", 0),), 1)

    def one_step(current, first_kernel, second_kernel):
        widened = rim_wide(current.astype(jnp.bfloat16))
        hidden = (gate_wide.astype(jnp.float32) * convolve_padded(widened, first_kernel)).astype(
            jnp.bfloat16
        )
        return current + convolve_padded(hidden, second_kernel)

    def backward_model(current):
        for step_index in range(STEPS):
            current = jnp.where(
                step_index < own_count, one_step(current, back_out, back_in), current
            )
        return current

    def observe_adjoint(scaled, like):
        tile_table = (
            jnp.zeros((like.size // TILE, TILE), jnp.float32)
            .at[tile_index]
            .add(weights * scaled[:, None])
        )
        return tile_table.reshape(like.shape)

    first_weighted = precision * departures[0]
    rhs = first_weighted + backward_model(
        observe_adjoint(obs_scale * innovation, first_weighted) - shift_up(first_weighted)
    )
    increment = jnp.zeros_like(rhs)
    residual = rhs
    direction = rhs
    norm_now = global_squares(residual)
    for iteration in range(ITERS):
        forward_current = direction
        for forward_step_index in range(STEPS):
            forward_current = jnp.where(
                forward_step_index < own_count,
                one_step(forward_current, conv_in, conv_out),
                forward_current,
            )
        earlier = from_behind(forward_current.astype(jnp.bfloat16), "tm", 1).astype(
            forward_current.dtype
        )
        misfit = direction - earlier
        weighted = precision * misfit
        picked = forward_current.reshape(-1, TILE)[tile_index]
        observed = jnp.sum(picked * weights, axis=1)
        apply_scaled = obs_scale * observed
        operator_image = weighted + backward_model(
            observe_adjoint(apply_scaled, direction) - shift_up(weighted)
        )
        curvature = lax.psum(jnp.sum(direction * operator_image), ("tm", "lat"))
        operator_image, curvature = (operator_image, curvature)
        step_length = norm_now / curvature
        increment = increment + step_length * direction
        residual = residual - step_length * operator_image
        norm_next = global_squares(residual)
        direction = residual + norm_next / norm_now * direction
        norm_now = norm_next
    return (increment[None], residual[None])


def solution(mesh):
    in_specs = (
        P(("ens", "tm"), "lat", None, None),
        P(("ens", "tm"), "lat", None, None),
        P(("ens", "tm"), "lat", None, None),
        P(),
        P(),
        P(),
        P(("ens", "tm")),
        P(("ens", "tm"), "lat"),
        P(("ens", "tm"), "lat", None),
        P(("ens", "tm"), "lat"),
        P(("ens", "tm"), "lat"),
    )
    out_specs = (P(("ens", "tm"), "lat", None, None), P(("ens", "tm"), "lat", None, None))
    return jax.shard_map(
        per_device, mesh=mesh, in_specs=in_specs, out_specs=out_specs, check_vma=False
    )
```

profile of v0, /device:TPU:0, one launch (start us, length us, event | category | flops | bytes accessed | tf_op | source)
XLA Modules:
  0.0 277.2 jit_solution(5226695543369262216)
XLA Ops:
  3.2 4.9 %collective-permute-start.1 = (bf16[1,69,256]{2,1,0:T(8,128)(2,1)S(1)}, bf16[1,69,256]{2,1,0:T(8,128)(2,1)S(1)}, u32[]{:S(2)}, u32[]{:S(2)}) collective-permute-start(bf16[1,69,256]{2,1,0:T(8,128)(2,1)S(1)} %get-tuple-element.80), channel_id=1, source_target_pairs={{0,1},{1,2},{2,3},{4,5},{5,6},{6,7},{8,9},{9,10},{10,11},{12,13},{... | collective-permute-start | bytes 105992 | tf_op jit(solution)/shard_map/ppermute | solution.py:19
  11.3 1.5 scatter_custom_fusion
  17.2 3.9 %collective-permute-start.5 = (bf16[2,69,256]{2,1,0:T(8,128)(2,1)S(1)}, bf16[2,69,256]{2,1,0:T(8,128)(2,1)S(1)}, u32[]{:S(2)}, u32[]{:S(2)}) collective-permute-start(bf16[2,69,256]{2,1,0:T(8,128)(2,1)S(1)} %fusion.374), channel_id=1, source_target_pairs={{0,1},{1,2},{2,3},{4,5},{5,6},{6,7},{8,9},{9,10},{10,11},{12,13},{... | collective-permute-start | bytes 211976 | tf_op jit(solution)/shard_map/ppermute | solution.py:19
  22.4 4.5 %collective-permute-start.3 = (bf16[1,128,256]{1,2,0:T(8,128)(2,1)S(1)}, bf16[1,128,256]{1,2,0:T(8,128)(2,1)S(1)}, u32[]{:S(2)}, u32[]{:S(2)}) collective-permute-start(bf16[1,128,256]{1,2,0:T(8,128)(2,1)S(1)} %get-tuple-element.78), channel_id=1, source_target_pairs={{0,1},{1,2},{2,3},{4,5},{5,6},{6,7},{8,9},{9,10},{10,11},{12,13},{... | collective-permute-start | bytes 196616 | tf_op jit(solution)/shard_map/ppermute | solution.py:19
  31.0 2.1 collective-permute-done.4
  35.4 3.5 %collective-permute-start.7 = (bf16[2,69,256]{2,1,0:T(8,128)(2,1)S(1)}, bf16[2,69,256]{2,1,0:T(8,128)(2,1)S(1)}, u32[]{:S(2)}, u32[]{:S(2)}) collective-permute-start(bf16[2,69,256]{2,1,0:T(8,128)(2,1)S(1)} %get-tuple-element.84), channel_id=1, source_target_pairs={{0,1},{1,2},{2,3},{4,5},{5,6},{6,7},{8,9},{9,10},{10,11},{12,13},{... | collective-permute-start | bytes 211976 | tf_op jit(solution)/shard_map/ppermute | solution.py:19
  40.8 4.3 %collective-permute-done.8 = bf16[2,69,256]{2,1,0:T(8,128)(2,1)S(1)} collective-permute-done((bf16[2,69,256]{2,1,0:T(8,128)(2,1)S(1)}, bf16[2,69,256]{2,1,0:T(8,128)(2,1)S(1)}, u32[]{:S(2)}, u32[]{:S(2)}) %collective-permute-start.8) | collective-permute-done | bytes 70688 | tf_op jit(solution)/shard_map/ppermute | solution.py:21
  50.9 3.5 %collective-permute-start.9 = (bf16[2,69,256]{2,1,0:T(8,128)(2,1)S(1)}, bf16[2,69,256]{2,1,0:T(8,128)(2,1)S(1)}, u32[]{:S(2)}, u32[]{:S(2)}) collective-permute-start(bf16[2,69,256]{2,1,0:T(8,128)(2,1)S(1)} %get-tuple-element.86), channel_id=1, source_target_pairs={{0,1},{1,2},{2,3},{4,5},{5,6},{6,7},{8,9},{9,10},{10,11},{12,13},{... | collective-permute-start | bytes 211976 | tf_op jit(solution)/shard_map/ppermute | solution.py:19
  56.4 4.3 %collective-permute-done.10 = bf16[2,69,256]{2,1,0:T(8,128)(2,1)S(1)} collective-permute-done((bf16[2,69,256]{2,1,0:T(8,128)(2,1)S(1)}, bf16[2,69,256]{2,1,0:T(8,128)(2,1)S(1)}, u32[]{:S(2)}, u32[]{:S(2)}) %collective-permute-start.10) | collective-permute-done | bytes 70688 | tf_op jit(solution)/shard_map/ppermute | solution.py:21
  65.7 2.5 collective-permute-start.11
  68.1 1.5 collective-permute-start.12
  70.1 4.3 %collective-permute-done.12 = bf16[2,69,256]{2,1,0:T(8,128)(2,1)S(1)} collective-permute-done((bf16[2,69,256]{2,1,0:T(8,128)(2,1)S(1)}, bf16[2,69,256]{2,1,0:T(8,128)(2,1)S(1)}, u32[]{:S(2)}, u32[]{:S(2)}) %collective-permute-start.12) | collective-permute-done | bytes 70688 | tf_op jit(solution)/shard_map/ppermute | solution.py:21
  83.0 1.5 scatter_custom_fusion.1
  84.6 3.0 %collective-permute-done.14 = bf16[2,69,256]{2,1,0:T(8,128)(2,1)S(1)} collective-permute-done((bf16[2,69,256]{2,1,0:T(8,128)(2,1)S(1)}, bf16[2,69,256]{2,1,0:T(8,128)(2,1)S(1)}, u32[]{:S(2)}, u32[]{:S(2)}) %collective-permute-start.14) | collective-permute-done | bytes 70688 | tf_op jit(solution)/shard_map/ppermute | solution.py:31
  87.6 1.9 collective-permute-start.15
  91.5 4.3 %collective-permute-done.16 = bf16[2,69,256]{2,1,0:T(8,128)(2,1)S(1)} collective-permute-done((bf16[2,69,256]{2,1,0:T(8,128)(2,1)S(1)}, bf16[2,69,256]{2,1,0:T(8,128)(2,1)S(1)}, u32[]{:S(2)}, u32[]{:S(2)}) %collective-permute-start.16) | collective-permute-done | bytes 70688 | tf_op jit(solution)/shard_map/ppermute | solution.py:21
  100.8 1.9 collective-permute-start.17
  104.7 4.3 %collective-permute-done.18 = bf16[2,69,256]{2,1,0:T(8,128)(2,1)S(1)} collective-permute-done((bf16[2,69,256]{2,1,0:T(8,128)(2,1)S(1)}, bf16[2,69,256]{2,1,0:T(8,128)(2,1)S(1)}, u32[]{:S(2)}, u32[]{:S(2)}) %collective-permute-start.18) | collective-permute-done | bytes 70688 | tf_op jit(solution)/shard_map/ppermute | solution.py:21
  114.7 30.4 %all-reduce = (f32[]{:T(128)}, f32[]{:T(128)}) all-reduce(f32[]{:T(128)} %get-tuple-element.7, f32[]{:T(128)} %get-tuple-element.6), channel_id=1, replica_groups=mesh['ens'=2,'tm'=4,'lat'=4] {'tm','lat'}, use_global_device_ids=true, to_apply=%region_2.3 | all-reduce | flops 2 | bytes 16 | tf_op jit(solution)/shard_map/psum | solution.py:62
  147.0 32.6 %psum.30 = f32[]{:T(128)} all-reduce(f32[]{:T(128)} %multiply_reduce_fusion.1), channel_id=1, replica_groups=mesh['ens'=2,'tm'=4,'lat'=4] {'tm','lat'}, use_global_device_ids=true, to_apply=%region_8.9 | all-reduce | flops 1 | bytes 8 | tf_op jit(solution)/shard_map/psum | solution.py:62
  180.9 1.9 collective-permute-start.19
  184.7 4.3 %collective-permute-done.20 = bf16[2,69,256]{2,1,0:T(8,128)(2,1)S(1)} collective-permute-done((bf16[2,69,256]{2,1,0:T(8,128)(2,1)S(1)}, bf16[2,69,256]{2,1,0:T(8,128)(2,1)S(1)}, u32[]{:S(2)}, u32[]{:S(2)}) %collective-permute-start.20) | collective-permute-done | bytes 70688 | tf_op jit(solution)/shard_map/ppermute | solution.py:21
  194.0 2.8 collective-permute-start.21
  196.8 1.5 collective-permute-start.22
  198.8 4.3 %collective-permute-done.22 = bf16[2,69,256]{2,1,0:T(8,128)(2,1)S(1)} collective-permute-done((bf16[2,69,256]{2,1,0:T(8,128)(2,1)S(1)}, bf16[2,69,256]{2,1,0:T(8,128)(2,1)S(1)}, u32[]{:S(2)}, u32[]{:S(2)}) %collective-permute-start.22) | collective-permute-done | bytes 70688 | tf_op jit(solution)/shard_map/ppermute | solution.py:21
  211.7 1.5 scatter_custom_fusion.2
  213.3 3.7 %collective-permute-done.24 = bf16[2,69,256]{2,1,0:T(8,128)(2,1)S(1)} collective-permute-done((bf16[2,69,256]{2,1,0:T(8,128)(2,1)S(1)}, bf16[2,69,256]{2,1,0:T(8,128)(2,1)S(1)}, u32[]{:S(2)}, u32[]{:S(2)}) %collective-permute-start.24) | collective-permute-done | bytes 70688 | tf_op jit(solution)/shard_map/ppermute | solution.py:31
  217.0 2.0 collective-permute-start.25
  220.9 4.3 %collective-permute-done.26 = bf16[2,69,256]{2,1,0:T(8,128)(2,1)S(1)} collective-permute-done((bf16[2,69,256]{2,1,0:T(8,128)(2,1)S(1)}, bf16[2,69,256]{2,1,0:T(8,128)(2,1)S(1)}, u32[]{:S(2)}, u32[]{:S(2)}) %collective-permute-start.26) | collective-permute-done | bytes 70688 | tf_op jit(solution)/shard_map/ppermute | solution.py:21
  230.2 1.9 collective-permute-start.27
  234.1 4.3 %collective-permute-done.28 = bf16[2,69,256]{2,1,0:T(8,128)(2,1)S(1)} collective-permute-done((bf16[2,69,256]{2,1,0:T(8,128)(2,1)S(1)}, bf16[2,69,256]{2,1,0:T(8,128)(2,1)S(1)}, u32[]{:S(2)}, u32[]{:S(2)}) %collective-permute-start.28) | collective-permute-done | bytes 70688 | tf_op jit(solution)/shard_map/ppermute | solution.py:21
  244.0 30.3 %psum.31 = f32[]{:T(128)} all-reduce(f32[]{:T(128)} %get-tuple-element.101), channel_id=1, replica_groups=mesh['ens'=2,'tm'=4,'lat'=4] {'tm','lat'}, use_global_device_ids=true, to_apply=%region_12.13 | all-reduce | flops 1 | bytes 8 | tf_op jit(solution)/shard_map/psum | solution.py:141
  (314 shorter events, 87.2 us)
Async XLA Ops:
  0.6 2.5 copy-start.5
  1.7 7.8 %copy-start.2 = (bf16[3,3,69,128]{3,2,1,0:T(8,128)(2,1)S(1)}, bf16[3,3,69,128]{3,2,1,0:T(8,128)(2,1)}, u32[]{:S(2)}) copy-start(bf16[3,3,69,128]{3,2,1,0:T(8,128)(2,1)} %param.15) | copy-start | bytes 476932
  1.7 15.5 %collective-permute-start = (bf16[2,69,256]{2,1,0:T(8,128)(2,1)S(1)}, bf16[2,69,256]{2,1,0:T(8,128)(2,1)S(1)}, u32[]{:S(2)}, u32[]{:S(2)}) collective-permute-start(bf16[2,69,256]{2,1,0:T(8,128)(2,1)S(1)} %fusion.390), channel_id=1, source_target_pairs={{4,0},{8,4},{12,8},{5,1},{9,5},{13,9},{6,2},{10,6},{14,10},{7,3},{... | collective-permute-start | bytes 211976 | tf_op jit(solution)/shard_map/ppermute | solution.py:31
  3.2 6.3 %copy-start.8 = (s32[1,256]{1,0:T(1,128)S(1)}, s32[1,256]{1,0:T(1,128)}, u32[]{:S(2)}) copy-start(s32[1,256]{1,0:T(1,128)} %param.18) | copy-start | bytes 3076
  3.2 10.4 %collective-permute-start.1 = (bf16[1,69,256]{2,1,0:T(8,128)(2,1)S(1)}, bf16[1,69,256]{2,1,0:T(8,128)(2,1)S(1)}, u32[]{:S(2)}, u32[]{:S(2)}) collective-permute-start(bf16[1,69,256]{2,1,0:T(8,128)(2,1)S(1)} %get-tuple-element.80), channel_id=1, source_target_pairs={{0,1},{1,2},{2,3},{4,5},{5,6},{6,7},{8,9},{9,10},{10,11},{12,13},{... | collective-permute-start | bytes 105992 | tf_op jit(solution)/shard_map/ppermute | solution.py:19
  8.1 6.1 %collective-permute-start.2 = (bf16[1,69,256]{2,1,0:T(8,128)(2,1)S(1)}, bf16[1,69,256]{2,1,0:T(8,128)(2,1)S(1)}, u32[]{:S(2)}, u32[]{:S(2)}) collective-permute-start(bf16[1,69,256]{2,1,0:T(8,128)(2,1)S(1)} %get-tuple-element.81), channel_id=1, source_target_pairs={{1,0},{2,1},{3,2},{5,4},{6,5},{7,6},{9,8},{10,9},{11,10},{13,12},{... | collective-permute-start | bytes 105992 | tf_op jit(solution)/shard_map/ppermute | solution.py:21
  17.2 11.1 %collective-permute-start.5 = (bf16[2,69,256]{2,1,0:T(8,128)(2,1)S(1)}, bf16[2,69,256]{2,1,0:T(8,128)(2,1)S(1)}, u32[]{:S(2)}, u32[]{:S(2)}) collective-permute-start(bf16[2,69,256]{2,1,0:T(8,128)(2,1)S(1)} %fusion.374), channel_id=1, source_target_pairs={{0,1},{1,2},{2,3},{4,5},{5,6},{6,7},{8,9},{9,10},{10,11},{12,13},{... | collective-permute-start | bytes 211976 | tf_op jit(solution)/shard_map/ppermute | solution.py:19
  21.1 7.2 %collective-permute-start.6 = (bf16[2,69,256]{2,1,0:T(8,128)(2,1)S(1)}, bf16[2,69,256]{2,1,0:T(8,128)(2,1)S(1)}, u32[]{:S(2)}, u32[]{:S(2)}) collective-permute-start(bf16[2,69,256]{2,1,0:T(8,128)(2,1)S(1)} %fusion.374), channel_id=1, source_target_pairs={{1,0},{2,1},{3,2},{5,4},{6,5},{7,6},{9,8},{10,9},{11,10},{13,12},{... | collective-permute-start | bytes 211976 | tf_op jit(solution)/shard_map/ppermute | solution.py:21
  22.4 8.6 %collective-permute-start.3 = (bf16[1,128,256]{1,2,0:T(8,128)(2,1)S(1)}, bf16[1,128,256]{1,2,0:T(8,128)(2,1)S(1)}, u32[]{:S(2)}, u32[]{:S(2)}) collective-permute-start(bf16[1,128,256]{1,2,0:T(8,128)(2,1)S(1)} %get-tuple-element.78), channel_id=1, source_target_pairs={{0,1},{1,2},{2,3},{4,5},{5,6},{6,7},{8,9},{9,10},{10,11},{12,13},{... | collective-permute-start | bytes 196616 | tf_op jit(solution)/shard_map/ppermute | solution.py:19
  27.0 6.2 %collective-permute-start.4 = (bf16[1,128,256]{1,2,0:T(8,128)(2,1)S(1)}, bf16[1,128,256]{1,2,0:T(8,128)(2,1)S(1)}, u32[]{:S(2)}, u32[]{:S(2)}) collective-permute-start(bf16[1,128,256]{1,2,0:T(8,128)(2,1)S(1)} %get-tuple-element.79), channel_id=1, source_target_pairs={{1,0},{2,1},{3,2},{5,4},{6,5},{7,6},{9,8},{10,9},{11,10},{13,12},{... | collective-permute-start | bytes 196616 | tf_op jit(solution)/shard_map/ppermute | solution.py:21
  35.4 5.5 %collective-permute-start.7 = (bf16[2,69,256]{2,1,0:T(8,128)(2,1)S(1)}, bf16[2,69,256]{2,1,0:T(8,128)(2,1)S(1)}, u32[]{:S(2)}, u32[]{:S(2)}) collective-permute-start(bf16[2,69,256]{2,1,0:T(8,128)(2,1)S(1)} %get-tuple-element.84), channel_id=1, source_target_pairs={{0,1},{1,2},{2,3},{4,5},{5,6},{6,7},{8,9},{9,10},{10,11},{12,13},{... | collective-permute-start | bytes 211976 | tf_op jit(solution)/shard_map/ppermute | solution.py:19
  38.9 6.2 %collective-permute-start.8 = (bf16[2,69,256]{2,1,0:T(8,128)(2,1)S(1)}, bf16[2,69,256]{2,1,0:T(8,128)(2,1)S(1)}, u32[]{:S(2)}, u32[]{:S(2)}) collective-permute-start(bf16[2,69,256]{2,1,0:T(8,128)(2,1)S(1)} %get-tuple-element.84), channel_id=1, source_target_pairs={{1,0},{2,1},{3,2},{5,4},{6,5},{7,6},{9,8},{10,9},{11,10},{13,12},{... | collective-permute-start | bytes 211976 | tf_op jit(solution)/shard_map/ppermute | solution.py:21
  50.9 5.5 %collective-permute-start.9 = (bf16[2,69,256]{2,1,0:T(8,128)(2,1)S(1)}, bf16[2,69,256]{2,1,0:T(8,128)(2,1)S(1)}, u32[]{:S(2)}, u32[]{:S(2)}) collective-permute-start(bf16[2,69,256]{2,1,0:T(8,128)(2,1)S(1)} %get-tuple-element.86), channel_id=1, source_target_pairs={{0,1},{1,2},{2,3},{4,5},{5,6},{6,7},{8,9},{9,10},{10,11},{12,13},{... | collective-permute-start | bytes 211976 | tf_op jit(solution)/shard_map/ppermute | solution.py:19
  54.4 6.2 %collective-permute-start.10 = (bf16[2,69,256]{2,1,0:T(8,128)(2,1)S(1)}, bf16[2,69,256]{2,1,0:T(8,128)(2,1)S(1)}, u32[]{:S(2)}, u32[]{:S(2)}) collective-permute-start(bf16[2,69,256]{2,1,0:T(8,128)(2,1)S(1)} %get-tuple-element.86), channel_id=1, source_target_pairs={{1,0},{2,1},{3,2},{5,4},{6,5},{7,6},{9,8},{10,9},{11,10},{13,12},{... | collective-permute-start | bytes 211976 | tf_op jit(solution)/shard_map/ppermute | solution.py:21
  65.7 4.5 %collective-permute-start.11 = (bf16[2,69,256]{2,1,0:T(8,128)(2,1)S(1)}, bf16[2,69,256]{2,1,0:T(8,128)(2,1)S(1)}, u32[]{:S(2)}, u32[]{:S(2)}) collective-permute-start(bf16[2,69,256]{2,1,0:T(8,128)(2,1)S(1)} %get-tuple-element.88), channel_id=1, source_target_pairs={{0,1},{1,2},{2,3},{4,5},{5,6},{6,7},{8,9},{9,10},{10,11},{12,13},{... | collective-permute-start | bytes 211976 | tf_op jit(solution)/shard_map/ppermute | solution.py:19
  68.1 6.2 %collective-permute-start.12 = (bf16[2,69,256]{2,1,0:T(8,128)(2,1)S(1)}, bf16[2,69,256]{2,1,0:T(8,128)(2,1)S(1)}, u32[]{:S(2)}, u32[]{:S(2)}) collective-permute-start(bf16[2,69,256]{2,1,0:T(8,128)(2,1)S(1)} %get-tuple-element.88), channel_id=1, source_target_pairs={{1,0},{2,1},{3,2},{5,4},{6,5},{7,6},{9,8},{10,9},{11,10},{13,12},{... | collective-permute-start | bytes 211976 | tf_op jit(solution)/shard_map/ppermute | solution.py:21
  79.4 2.2 collective-permute-start.13
  81.6 6.0 %collective-permute-start.14 = (bf16[2,69,256]{2,1,0:T(8,128)(2,1)S(1)}, bf16[2,69,256]{2,1,0:T(8,128)(2,1)S(1)}, u32[]{:S(2)}, u32[]{:S(2)}) collective-permute-start(bf16[2,69,256]{2,1,0:T(8,128)(2,1)S(1)} %fusion.472), channel_id=1, source_target_pairs={{4,0},{8,4},{12,8},{5,1},{9,5},{13,9},{6,2},{10,6},{14,10},{7,3},{... | collective-permute-start | bytes 211976 | tf_op jit(solution)/shard_map/ppermute | solution.py:31
  87.6 3.9 %collective-permute-start.15 = (bf16[2,69,256]{2,1,0:T(8,128)(2,1)S(1)}, bf16[2,69,256]{2,1,0:T(8,128)(2,1)S(1)}, u32[]{:S(2)}, u32[]{:S(2)}) collective-permute-start(bf16[2,69,256]{2,1,0:T(8,128)(2,1)S(1)} %fusion.375), channel_id=1, source_target_pairs={{0,1},{1,2},{2,3},{4,5},{5,6},{6,7},{8,9},{9,10},{10,11},{12,13},{... | collective-permute-start | bytes 211976 | tf_op jit(solution)/shard_map/ppermute | solution.py:19
  89.6 6.2 %collective-permute-start.16 = (bf16[2,69,256]{2,1,0:T(8,128)(2,1)S(1)}, bf16[2,69,256]{2,1,0:T(8,128)(2,1)S(1)}, u32[]{:S(2)}, u32[]{:S(2)}) collective-permute-start(bf16[2,69,256]{2,1,0:T(8,128)(2,1)S(1)} %fusion.375), channel_id=1, source_target_pairs={{1,0},{2,1},{3,2},{5,4},{6,5},{7,6},{9,8},{10,9},{11,10},{13,12},{... | collective-permute-start | bytes 211976 | tf_op jit(solution)/shard_map/ppermute | solution.py:21
  100.8 3.9 %collective-permute-start.17 = (bf16[2,69,256]{2,1,0:T(8,128)(2,1)S(1)}, bf16[2,69,256]{2,1,0:T(8,128)(2,1)S(1)}, u32[]{:S(2)}, u32[]{:S(2)}) collective-permute-start(bf16[2,69,256]{2,1,0:T(8,128)(2,1)S(1)} %get-tuple-element.92), channel_id=1, source_target_pairs={{0,1},{1,2},{2,3},{4,5},{5,6},{6,7},{8,9},{9,10},{10,11},{12,13},{... | collective-permute-start | bytes 211976 | tf_op jit(solution)/shard_map/ppermute | solution.py:19
  102.8 6.2 %collective-permute-start.18 = (bf16[2,69,256]{2,1,0:T(8,128)(2,1)S(1)}, bf16[2,69,256]{2,1,0:T(8,128)(2,1)S(1)}, u32[]{:S(2)}, u32[]{:S(2)}) collective-permute-start(bf16[2,69,256]{2,1,0:T(8,128)(2,1)S(1)} %get-tuple-element.92), channel_id=1, source_target_pairs={{1,0},{2,1},{3,2},{5,4},{6,5},{7,6},{9,8},{10,9},{11,10},{13,12},{... | collective-permute-start | bytes 211976 | tf_op jit(solution)/shard_map/ppermute | solution.py:21
  180.9 3.8 %collective-permute-start.19 = (bf16[2,69,256]{2,1,0:T(8,128)(2,1)S(1)}, bf16[2,69,256]{2,1,0:T(8,128)(2,1)S(1)}, u32[]{:S(2)}, u32[]{:S(2)}) collective-permute-start(bf16[2,69,256]{2,1,0:T(8,128)(2,1)S(1)} %get-tuple-element.10), channel_id=1, source_target_pairs={{0,1},{1,2},{2,3},{4,5},{5,6},{6,7},{8,9},{9,10},{10,11},{12,13},{... | collective-permute-start | bytes 211976 | tf_op jit(solution)/shard_map/ppermute | solution.py:19
  182.8 6.2 %collective-permute-start.20 = (bf16[2,69,256]{2,1,0:T(8,128)(2,1)S(1)}, bf16[2,69,256]{2,1,0:T(8,128)(2,1)S(1)}, u32[]{:S(2)}, u32[]{:S(2)}) collective-permute-start(bf16[2,69,256]{2,1,0:T(8,128)(2,1)S(1)} %get-tuple-element.10), channel_id=1, source_target_pairs={{1,0},{2,1},{3,2},{5,4},{6,5},{7,6},{9,8},{10,9},{11,10},{13,12},{... | collective-permute-start | bytes 211976 | tf_op jit(solution)/shard_map/ppermute | solution.py:21
  194.0 4.7 %collective-permute-start.21 = (bf16[2,69,256]{2,1,0:T(8,128)(2,1)S(1)}, bf16[2,69,256]{2,1,0:T(8,128)(2,1)S(1)}, u32[]{:S(2)}, u32[]{:S(2)}) collective-permute-start(bf16[2,69,256]{2,1,0:T(8,128)(2,1)S(1)} %get-tuple-element.95), channel_id=1, source_target_pairs={{0,1},{1,2},{2,3},{4,5},{5,6},{6,7},{8,9},{9,10},{10,11},{12,13},{... | collective-permute-start | bytes 211976 | tf_op jit(solution)/shard_map/ppermute | solution.py:19
  196.8 6.2 %collective-permute-start.22 = (bf16[2,69,256]{2,1,0:T(8,128)(2,1)S(1)}, bf16[2,69,256]{2,1,0:T(8,128)(2,1)S(1)}, u32[]{:S(2)}, u32[]{:S(2)}) collective-permute-start(bf16[2,69,256]{2,1,0:T(8,128)(2,1)S(1)} %get-tuple-element.95), channel_id=1, source_target_pairs={{1,0},{2,1},{3,2},{5,4},{6,5},{7,6},{9,8},{10,9},{11,10},{13,12},{... | collective-permute-start | bytes 211976 | tf_op jit(solution)/shard_map/ppermute | solution.py:21
  208.1 2.2 collective-permute-start.23
  210.3 6.7 %collective-permute-start.24 = (bf16[2,69,256]{2,1,0:T(8,128)(2,1)S(1)}, bf16[2,69,256]{2,1,0:T(8,128)(2,1)S(1)}, u32[]{:S(2)}, u32[]{:S(2)}) collective-permute-start(bf16[2,69,256]{2,1,0:T(8,128)(2,1)S(1)} %fusion.473), channel_id=1, source_target_pairs={{4,0},{8,4},{12,8},{5,1},{9,5},{13,9},{6,2},{10,6},{14,10},{7,3},{... | collective-permute-start | bytes 211976 | tf_op jit(solution)/shard_map/ppermute | solution.py:31
  217.0 3.9 %collective-permute-start.25 = (bf16[2,69,256]{2,1,0:T(8,128)(2,1)S(1)}, bf16[2,69,256]{2,1,0:T(8,128)(2,1)S(1)}, u32[]{:S(2)}, u32[]{:S(2)}) collective-permute-start(bf16[2,69,256]{2,1,0:T(8,128)(2,1)S(1)} %fusion.376), channel_id=1, source_target_pairs={{0,1},{1,2},{2,3},{4,5},{5,6},{6,7},{8,9},{9,10},{10,11},{12,13},{... | collective-permute-start | bytes 211976 | tf_op jit(solution)/shard_map/ppermute | solution.py:19
  219.0 6.2 %collective-permute-start.26 = (bf16[2,69,256]{2,1,0:T(8,128)(2,1)S(1)}, bf16[2,69,256]{2,1,0:T(8,128)(2,1)S(1)}, u32[]{:S(2)}, u32[]{:S(2)}) collective-permute-start(bf16[2,69,256]{2,1,0:T(8,128)(2,1)S(1)} %fusion.376), channel_id=1, source_target_pairs={{1,0},{2,1},{3,2},{5,4},{6,5},{7,6},{9,8},{10,9},{11,10},{13,12},{... | collective-permute-start | bytes 211976 | tf_op jit(solution)/shard_map/ppermute | solution.py:21
  230.2 3.9 %collective-permute-start.27 = (bf16[2,69,256]{2,1,0:T(8,128)(2,1)S(1)}, bf16[2,69,256]{2,1,0:T(8,128)(2,1)S(1)}, u32[]{:S(2)}, u32[]{:S(2)}) collective-permute-start(bf16[2,69,256]{2,1,0:T(8,128)(2,1)S(1)} %get-tuple-element.99), channel_id=1, source_target_pairs={{0,1},{1,2},{2,3},{4,5},{5,6},{6,7},{8,9},{9,10},{10,11},{12,13},{... | collective-permute-start | bytes 211976 | tf_op jit(solution)/shard_map/ppermute | solution.py:19
  232.2 6.2 %collective-permute-start.28 = (bf16[2,69,256]{2,1,0:T(8,128)(2,1)S(1)}, bf16[2,69,256]{2,1,0:T(8,128)(2,1)S(1)}, u32[]{:S(2)}, u32[]{:S(2)}) collective-permute-start(bf16[2,69,256]{2,1,0:T(8,128)(2,1)S(1)} %get-tuple-element.99), channel_id=1, source_target_pairs={{1,0},{2,1},{3,2},{5,4},{6,5},{7,6},{9,8},{10,9},{11,10},{13,12},{... | collective-permute-start | bytes 211976 | tf_op jit(solution)/shard_map/ppermute | solution.py:21
  (7 other events, 5.8 us)
where the time goes:
time: 280 us; the launch traced here: 277 us
  blocking collectives  93.3 us (33%)
  starting transfers between devices  57.7 us (21%)
  waiting for transfers between devices  53.8 us (19%)
  matrix products  49.5 us (18%)
  other arithmetic  9.01 us (3%)
  local copies, waits for them, and re-layouts  7.35 us (3%)
  between operations  6.59 us (2%)
    psum x2, blocking collectives, global_squares(): return lax.psum(jnp.sum(source * source), ('tm', 'lat'))  63 us
    dot_general x189, matrix products, convolve_padded(): jnp.einsum('oi,ril->rol', kernel[row_off, col_off], window, preferred_ele...  49.5 us
    ppermute x12, waiting for transfers between devices, padded_2(): lax.ppermute(head, axis, [((i + 1) % count, i) for i in range(ends)])  41.3 us
    ppermute x12, starting transfers between devices, padded_2(): lax.ppermute(tail, axis, [(i, (i + 1) % count) for i in range(ends)])  35.2 us
    psum x1, blocking collectives, per_device(): curvature = lax.psum(jnp.sum(direction * operator_image), ('tm', 'lat'))  30.3 us
    ppermute x12, starting transfers between devices, padded_2(): lax.ppermute(head, axis, [((i + 1) % count, i) for i in range(ends)])  15.9 us
    ppermute x5, waiting for transfers between devices, from_behind(): lax.ppermute(value, axis, [(source, source + steps) for source in range(l...  6.94 us
    ppermute x5, starting transfers between devices, from_behind(): lax.ppermute(value, axis, [(source, source + steps) for source in range(l...  6.6 us
  transfers between devices with their start and end apart: 29, of which 24 were waited for; matrix products, arithmetic and copies ran while one was open for 4% of the time, Pallas kernels for 0%

commit v1 on v0

v1 whole, which is shorter than its diff:
```python
import functools

import jax
import jax.numpy as jnp
from jax import lax
from jax.experimental import pallas as pl
from jax.experimental.pallas import tpu as pltpu
from jax.sharding import PartitionSpec as P

TILE = 128
STEPS = 2
ITERS = 2
F32 = jnp.float32
BF16 = jnp.bfloat16


def padded_2(cells, sides, width):
    for axis, dim in sides:
        count = lax.axis_size(axis)
        ends = count - 1
        head = lax.slice_in_dim(cells, 0, width, axis=dim)
        tail = lax.slice_in_dim(cells, cells.shape[dim] - width, cells.shape[dim], axis=dim)
        cells = jnp.concatenate(
            [
                lax.ppermute(tail, axis, [(i, (i + 1) % count) for i in range(ends)]),
                cells,
                lax.ppermute(head, axis, [((i + 1) % count, i) for i in range(ends)]),
            ],
            axis=dim,
        )
    return cells


def from_behind(value, axis, steps):
    count = lax.axis_size(axis)
    leading, last = (max(0, -steps), min(count, count - steps))
    return lax.ppermute(value, axis, [(source, source + steps) for source in range(leading, last)])


def convolve_padded(padded, kernel):
    out_rows = padded.shape[0] - 2
    lon_len = padded.shape[2]
    wrapped = jnp.concatenate([padded[:, :, -1:], padded, padded[:, :, :1]], axis=2)
    accumulated = None
    for row_off in range(3):
        for col_off in range(3):
            window = wrapped[row_off : row_off + out_rows, :, col_off : col_off + lon_len]
            term = jnp.einsum(
                "oi,ril->rol", kernel[row_off, col_off], window, preferred_element_type=F32
            )
            accumulated = term if accumulated is None else accumulated + term
    return accumulated


def flipped(kernel):
    return jnp.transpose(kernel[::-1, ::-1], (0, 1, 3, 2))


def rim_wide(source):
    return padded_2(source, (("lat", 0),), 2)


def shift_up(source):
    return from_behind(source.astype(BF16), "tm", -1).astype(source.dtype)


def global_squares(source):
    return lax.psum(jnp.sum(source * source), ("tm", "lat"))


def halo_plan(
    departures,
    error_precision,
    trajectory,
    conv_in,
    conv_out,
    hidden_bias,
    step_counts,
    obs_tiles,
    obs_weights,
    innovations,
    obs_precision,
):
    precision = error_precision[0]
    own_count = step_counts[0]
    tile_index = obs_tiles[0]
    weights = obs_weights[0]
    innovation = innovations[0]
    obs_scale = obs_precision[0]
    back_in = flipped(conv_in)
    back_out = flipped(conv_out)
    trajectory_ext = padded_2(trajectory[0], (("lat", 0),), 1)
    gate_factor = (
        1.0 - jnp.tanh(convolve_padded(trajectory_ext, conv_in) + hidden_bias[:, None]) ** 2
    ).astype(BF16)
    gate_wide = padded_2(gate_factor, (("lat", 0),), 1)

    def one_step(current, first_kernel, second_kernel):
        widened = rim_wide(current.astype(BF16))
        hidden = (gate_wide.astype(F32) * convolve_padded(widened, first_kernel)).astype(BF16)
        return current + convolve_padded(hidden, second_kernel)

    def model(current, first_kernel, second_kernel):
        for step_index in range(STEPS):
            current = jnp.where(
                step_index < own_count, one_step(current, first_kernel, second_kernel), current
            )
        return current

    def observe_adjoint(scaled, like):
        tile_table = (
            jnp.zeros((like.size // TILE, TILE), F32)
            .at[tile_index]
            .add(weights * scaled[:, None])
        )
        return tile_table.reshape(like.shape)

    first_weighted = precision * departures[0]
    rhs = first_weighted + model(
        observe_adjoint(obs_scale * innovation, first_weighted) - shift_up(first_weighted),
        back_out,
        back_in,
    )
    increment = jnp.zeros_like(rhs)
    residual = rhs
    direction = rhs
    norm_now = global_squares(residual)
    for _ in range(ITERS):
        propagated = model(direction, conv_in, conv_out)
        earlier = from_behind(propagated.astype(BF16), "tm", 1).astype(F32)
        weighted = precision * (direction - earlier)
        picked = propagated.reshape(-1, TILE)[tile_index]
        observed = jnp.sum(picked * weights, axis=1)
        operator_image = weighted + model(
            observe_adjoint(obs_scale * observed, direction) - shift_up(weighted),
            back_out,
            back_in,
        )
        curvature = lax.psum(jnp.sum(direction * operator_image), ("tm", "lat"))
        step_length = norm_now / curvature
        increment = increment + step_length * direction
        residual = residual - step_length * operator_image
        norm_next = global_squares(residual)
        direction = residual + norm_next / norm_now * direction
        norm_now = norm_next
    return (increment[None], residual[None])


BANDS = 4
CHAN = 72
CHAN_IN = 80
PAIR = 2 * CHAN
SLOTS = 4 * CHAN
EXTRA = 16


def row_of(ref, row):
    return ref[row // 2, (row % 2) * CHAN : (row % 2 + 1) * CHAN, :]


def taps_of(row):
    zeros = jnp.zeros((CHAN_IN - CHAN, row.shape[1]), F32)
    right = pltpu.roll(row, 1, axis=1)
    left = pltpu.roll(row, row.shape[1] - 1, axis=1)
    return jnp.concatenate([right, zeros, row, zeros, left, zeros], axis=0).astype(BF16)


def conv_rows(read_row, w_in, emit):
    rows = 2 * BANDS
    hid = w_in.shape[0] // 3
    sums = [None] * (rows + 1)
    for source in range(rows):
        part = jnp.dot(w_in[...], taps_of(read_row(source)), preferred_element_type=F32)
        for row_off in range(3):
            target = source + 1 - row_off
            if 0 <= target < rows:
                piece = part[row_off * hid : (row_off + 1) * hid]
                sums[target] = piece if sums[target] is None else sums[target] + piece
        if source >= 1:
            emit(source - 1, sums[source - 1])
            sums[source - 1] = None
    emit(rows - 1, sums[rows - 1])


def model_steps(field, gate, w_in, w_out, hidden, count):
    def one_step(_, carry):
        def gated(row, value):
            hidden[row] = (gate[row].astype(F32) * value).astype(BF16)

        conv_rows(lambda row: row_of(field, row), w_in, gated)
        sums = {}
        for pair in range(BANDS):
            stacked = hidden[2 * pair : 2 * pair + 2].reshape(-1, hidden.shape[2])
            part = jnp.dot(w_out[...], stacked, preferred_element_type=F32)
            for m in range(4):
                target = 2 * pair - 1 + m
                if 0 <= target < 2 * BANDS:
                    piece = part[m * 3 * CHAN : (m + 1) * 3 * CHAN]
                    sums[target] = sums[target] + piece if target in sums else piece
            done = [2 * pair - 1, 2 * pair] if pair < BANDS - 1 else [2 * pair - 1, 2 * pair, 2 * pair + 1]
            for target in done:
                if target < 0:
                    continue
                total = sums.pop(target)
                lon = total.shape[1]
                spread = (
                    pltpu.roll(total[:CHAN], 1, axis=1)
                    + total[CHAN : 2 * CHAN]
                    + pltpu.roll(total[2 * CHAN :], lon - 1, axis=1)
                )
                at = (target % 2) * CHAN
                field[target // 2, at : at + CHAN, :] = row_of(field, target) + spread
        return carry

    lax.fori_loop(0, jnp.minimum(count, STEPS), one_step, 0)


def split_16(value):
    high = value.astype(BF16)
    low = (value - high.astype(F32)).astype(BF16)
    return high, low


def extras_of(obs):
    return obs[TILE * 2 : TILE * 2 + EXTRA, :].astype(F32)


def slots_row(extra):
    halves = [2.0 * extra[h : h + 1] + extra[2 + h : 3 + h] for h in range(2)]
    return halves


def one_hot_t(halves):
    iota = lax.broadcasted_iota(jnp.int32, (SLOTS, TILE), 0).astype(F32)
    return jnp.concatenate([(iota == half).astype(F32) for half in halves], axis=1)


def one_hot(halves):
    columns = [
        jnp.transpose(jnp.broadcast_to(half, (TILE, TILE)))[:, :1] for half in halves
    ]
    column = jnp.concatenate(columns, axis=0)
    iota = lax.broadcasted_iota(jnp.int32, (2 * TILE, SLOTS), 1).astype(F32)
    return (iota == column).astype(F32)


def band_slots(band):
    return jnp.concatenate(
        [
            band[row * CHAN : (row + 1) * CHAN, half * TILE : (half + 1) * TILE]
            for row in range(2)
            for half in range(2)
        ],
        axis=0,
    )


def slots_band(slots):
    return jnp.concatenate(
        [
            jnp.concatenate(
                [slots[(2 * row + half) * CHAN : (2 * row + half + 1) * CHAN] for half in range(2)],
                axis=1,
            )
            for row in range(2)
        ],
        axis=0,
    )


def gate_kernel(t0, t1, t2, t3, w_in, bias, gate, field):
    me = lax.axis_index("lat")
    for shift, block in enumerate((t0, t1, t2, t3)):
        field[me ^ shift] = block[...].astype(F32)

    def emit(row, value):
        squashed = jnp.tanh(value + bias[...])
        gate[row] = (1.0 - squashed * squashed).astype(BF16)

    conv_rows(lambda row: row_of(field, row), w_in, emit)


def rhs_kernel(
    counts, y0, y1, y2, y3, later, o0, o1, o2, o3, gate, w_in, w_out, out, out_b, field, hidden
):
    me = lax.axis_index("lat")
    more = lax.axis_index("tm") < lax.axis_size("tm") - 1
    for shift, obs in enumerate((o0, o1, o2, o3)):
        extra = extras_of(obs)
        hot = one_hot_t(slots_row(extra))
        high = jnp.concatenate([extra[4:5], extra[5:6]], axis=1)
        low = jnp.concatenate([extra[6:7], extra[7:8]], axis=1)
        both = jnp.concatenate([hot * high, hot * low], axis=1).astype(BF16)
        weights = obs[: 2 * TILE, :]
        slots = jnp.dot(
            both, jnp.concatenate([weights, weights], axis=0), preferred_element_type=F32
        )
        next_y = jnp.where(more, later[shift].astype(F32), 0.0)
        field[me ^ shift] = slots_band(slots) - next_y
    model_steps(field, gate, w_in, w_out, hidden, counts[0])
    for shift, block in enumerate((y0, y1, y2, y3)):
        total = field[me ^ shift] + block[...].astype(F32)
        out[me ^ shift] = total
        out_b[me ^ shift] = total.astype(BF16)


def forward_kernel(counts, start, gate, w_in, w_out, out, out_b, hidden):
    out[...] = start[...]
    model_steps(out, gate, w_in, w_out, hidden, counts[0])
    out_b[...] = out[...].astype(BF16)


def observe_kernel(z, o0, o1, o2, o3, out):
    me = lax.axis_index("lat")
    for shift, obs in enumerate((o0, o1, o2, o3)):
        halves = slots_row(extras_of(obs))
        weights = obs[: 2 * TILE, :].astype(F32)
        high, low = split_16(band_slots(z[me ^ shift]))
        both = jnp.concatenate([high, low], axis=1)
        picked = jnp.dot(one_hot(halves).astype(BF16), both, preferred_element_type=F32)
        picked = picked[:, :TILE] + picked[:, TILE:]
        scaled = jnp.sum(picked * weights, axis=1, keepdims=True)
        high, low = split_16(weights * scaled)
        both = jnp.concatenate([high, low], axis=1)
        slots = jnp.dot(one_hot_t(halves).astype(BF16), both, preferred_element_type=F32)
        out[me ^ shift] = slots_band(slots[:, :TILE] + slots[:, TILE:])


def adjoint_kernel(
    counts, observed, z, later, p0, p1, p2, p3, gate, w_in, w_out, out, hidden
):
    me = lax.axis_index("lat")
    more = lax.axis_index("tm") < lax.axis_size("tm") - 1
    for shift, block in enumerate((p0, p1, p2, p3)):
        at = me ^ shift
        weight = jnp.where(more, block[...].astype(F32), 0.0)
        out[at] = observed[at] - weight * (later[at].astype(F32) - z[at])
    model_steps(out, gate, w_in, w_out, hidden, counts[0])


def image_of(at, tm_first, block, start, earlier, adjoint):
    before = jnp.where(tm_first, 0.0, earlier[at].astype(F32))
    return block[...].astype(F32) * (start[at] - before) + adjoint[at]


def image_kernel(start, earlier, adjoint, p0, p1, p2, p3, out, out_b):
    me = lax.axis_index("lat")
    tm_first = lax.axis_index("tm") == 0
    for shift, block in enumerate((p0, p1, p2, p3)):
        at = me ^ shift
        total = image_of(at, tm_first, block, start, earlier, adjoint)
        out[at] = total
        out_b[at] = total.astype(BF16)


def last_image_kernel(first, start, earlier, adjoint, p0, p1, p2, p3, own, dots):
    me = lax.axis_index("lat")
    tm_first = lax.axis_index("tm") == 0
    sums = [None] * 5
    for shift, block in enumerate((p0, p1, p2, p3)):
        at = me ^ shift
        total = image_of(at, tm_first, block, start, earlier, adjoint)
        if shift == 0:
            own[...] = total
        r0, v1 = first[at], start[at]
        for j, (a, b) in enumerate(((r0, r0), (r0, v1), (v1, v1), (r0, total), (v1, total))):
            piece = jnp.sum(a * b, axis=0, keepdims=True)
            sums[j] = piece if sums[j] is None else sums[j] + piece
    for j in range(5):
        value = jnp.sum(sums[j], axis=1, keepdims=True)
        dots[j : j + 1, :] = jnp.broadcast_to(value, (1, TILE))
    dots[5:8, :] = jnp.zeros((3, TILE), F32)


def finish_kernel(lat_at, d0, d1, d2, d3, first, second, third, inc, res):
    chan = inc.shape[1]
    lon = inc.shape[2]
    total = (d0[...] + d1[...]) + (d2[...] + d3[...])
    rr0, c0, g11, g02, g12 = [total[j : j + 1, :1] for j in range(5)]
    a0 = rr0 / c0
    rr1 = rr0 - 2.0 * a0 * c0 + a0 * a0 * g11
    beta = rr1 / rr0
    grow = 1.0 + beta
    c1 = grow * grow * c0 - grow * a0 * (g02 + g11) + a0 * a0 * g12
    a1 = rr1 / c1
    inc_r, inc_v = a0 + a1 * grow, -a1 * a0
    res_v1, res_v2 = -(a0 + a1 * grow), a1 * a0
    wide = lambda value: jnp.broadcast_to(value, (chan, lon))
    inc_r, inc_v, res_v1, res_v2 = wide(inc_r), wide(inc_v), wide(res_v1), wide(res_v2)
    for row in range(2):
        at = row * CHAN
        r0 = first[0, at : at + chan, :]
        v1 = second[0, at : at + chan, :]
        v2 = third[at : at + chan, :]
        inc[row] = inc_r * r0 + inc_v * v1
        res[row] = r0 + res_v1 * v1 + res_v2 * v2


VMEM = pl.BlockSpec(memory_space=pltpu.VMEM)
SMEM = pl.BlockSpec(memory_space=pltpu.SMEM)


def call(kernel, name, ins, outs, scratch=(), scalars=0):
    specs = [SMEM] * scalars + [VMEM] * (len(ins) - scalars)
    return pl.pallas_call(
        kernel,
        name=name,
        out_shape=outs,
        in_specs=specs,
        out_specs=[VMEM] * len(outs),
        scratch_shapes=list(scratch),
        compiler_params=pltpu.CompilerParams(vmem_limit_bytes=48 << 20),
    )(*ins)


def stack_in(kernel):
    rows, cols, out_c, in_c = kernel.shape
    padded = jnp.pad(kernel, ((0, 0), (0, 0), (0, 0), (0, CHAN_IN - in_c)))
    return jnp.transpose(padded, (0, 2, 1, 3)).reshape(rows * out_c, cols * CHAN_IN)


def stack_out(kernel):
    rows, cols, out_c, in_c = kernel.shape
    padded = jnp.pad(kernel, ((0, 0), (0, 0), (0, CHAN - out_c), (0, 0)))
    none = jnp.zeros_like(padded[0])
    tap = lambda row_off: padded[row_off] if 0 <= row_off < rows else none
    blocks = [jnp.concatenate([tap(2 - m), tap(3 - m)], axis=-1) for m in range(4)]
    return jnp.concatenate(blocks, axis=0).reshape(4 * cols * CHAN, 2 * in_c)


def as_band(cells):
    rows, chan, lon = cells.shape
    return jnp.pad(cells.astype(BF16), ((0, 0), (0, CHAN - chan), (0, 0))).reshape(PAIR, lon)


def by_partner(value):
    count = lax.axis_size("lat")
    blocks = [value]
    for shift in range(1, count):
        blocks.append(lax.ppermute(value, "lat", [(i, i ^ shift) for i in range(count)]))
    return blocks


def along_tm(value, step):
    count = lax.axis_size("tm")
    return lax.ppermute(value, "tm", [(i, (i + step) % count) for i in range(count)])


def row_plan(
    departures,
    error_precision,
    trajectory,
    conv_in,
    conv_out,
    hidden_bias,
    step_counts,
    obs_tiles,
    obs_weights,
    innovations,
    obs_precision,
):
    _, rows, chan, lon = departures.shape
    hid = conv_in.shape[2]
    shape = lambda *dims: jax.ShapeDtypeStruct(dims, F32)
    shape_b = lambda *dims: jax.ShapeDtypeStruct(dims, BF16)
    whole, whole_b = shape(BANDS, PAIR, lon), shape_b(BANDS, PAIR, lon)

    y_own = as_band(error_precision[0] * departures[0])
    y_all = by_partner(y_own)
    t_all = by_partner(as_band(trajectory[0]))

    root = jnp.sqrt(obs_precision[0])
    tiles = obs_tiles[0]
    per_row = 2 * chan
    slot = (2 * (tiles // per_row) + tiles % 2) * CHAN + (tiles // 2) % chan
    innov_high, innov_low = split_16(root * innovations[0])
    table = lambda value: value.astype(BF16).reshape(-1, TILE)
    obs_own = jnp.concatenate(
        [
            (obs_weights[0] * root[:, None]).astype(BF16),
            table(slot // 2),
            table(slot % 2),
            table(innov_high),
            table(innov_low),
            jnp.zeros((EXTRA - 8, TILE), BF16),
        ],
        axis=0,
    )
    o_all = by_partner(obs_own)
    p_all = by_partner(as_band(error_precision[0]))
    y_later = along_tm(jnp.stack(y_all), -1)
    p_later = [along_tm(block, -1) for block in p_all]

    fore_in, fore_out = stack_in(conv_in), stack_out(conv_out)
    back_in, back_out = stack_in(flipped(conv_out)), stack_out(flipped(conv_in))
    hidden = pltpu.VMEM((rows * BANDS, hid, lon), BF16)
    field = pltpu.VMEM((BANDS, PAIR, lon), F32)

    (gate,) = call(
        gate_kernel,
        "gate",
        (*t_all, fore_in, hidden_bias[:, None]),
        [shape_b(rows * BANDS, hid, lon)],
        [field],
    )
    r0, r0_b = call(
        rhs_kernel,
        "rhs",
        (step_counts, *y_all, y_later, *o_all, gate, back_in, back_out),
        [whole, whole_b],
        [field, hidden],
        1,
    )

    def half(start, start_b):
        later = along_tm(start_b, -1)
        z, z_b = call(
            forward_kernel,
            "forward",
            (step_counts, start, gate, fore_in, fore_out),
            [whole, whole_b],
            [hidden],
            1,
        )
        earlier = along_tm(z_b, 1)
        (observed,) = call(observe_kernel, "observe", (z, *o_all), [whole])
        (adjoint,) = call(
            adjoint_kernel,
            "adjoint",
            (step_counts, observed, z, later, *p_later, gate, back_in, back_out),
            [whole],
            [hidden],
            1,
        )
        return earlier, adjoint

    earlier, adjoint = half(r0, r0_b)
    v1, v1_b = call(image_kernel, "image", (r0, earlier, adjoint, *p_all), [whole, whole_b])
    earlier, adjoint = half(v1, v1_b)
    own, dots = call(
        last_image_kernel,
        "last_image",
        (r0, v1, earlier, adjoint, *p_all),
        [shape(PAIR, lon), shape(8, TILE)],
    )
    count = lax.axis_size("tm")
    parts = [dots] + [
        lax.ppermute(dots, "tm", [(i, i ^ step) for i in range(count)]) for step in range(1, count)
    ]
    at = lax.axis_index("lat").astype(jnp.int32).reshape(1)
    small = pl.BlockSpec((8, TILE), lambda g, lat_at: (0, 0))
    band = pl.BlockSpec((1, PAIR, lon), lambda g, lat_at: (lat_at[0], 0, 0))
    out_block = pl.BlockSpec((rows, chan, lon), lambda g, lat_at: (0, 0, 0))
    inc, res = pl.pallas_call(
        finish_kernel,
        name="finish",
        grid_spec=pltpu.PrefetchScalarGridSpec(
            num_scalar_prefetch=1,
            grid=(1,),
            in_specs=[small] * 4 + [band, band, pl.BlockSpec((PAIR, lon), lambda g, lat_at: (0, 0))],
            out_specs=[out_block, out_block],
        ),
        out_shape=[shape(rows, chan, lon)] * 2,
    )(at, *parts, r0, v1, own)
    return (inc[None], res[None])


def solution(mesh):
    in_specs = (
        P(("ens", "tm"), "lat", None, None),
        P(("ens", "tm"), "lat", None, None),
        P(("ens", "tm"), "lat", None, None),
        P(),
        P(),
        P(),
        P(("ens", "tm")),
        P(("ens", "tm"), "lat"),
        P(("ens", "tm"), "lat", None),
        P(("ens", "tm"), "lat"),
        P(("ens", "tm"), "lat"),
    )
    out_specs = (P(("ens", "tm"), "lat", None, None), P(("ens", "tm"), "lat", None, None))
    plan = row_plan if mesh.shape["lat"] == BANDS and mesh.shape["tm"] == 4 else halo_plan
    return jax.shard_map(plan, mesh=mesh, in_specs=in_specs, out_specs=out_specs, check_vma=False)
```

time: 280 us -> 82.2 us (0.29); the launches traced: 277 us -> 82.5 us
  blocking collectives: 93.3 us -> 0 us
  matrix products: 49.5 us -> 0 us
  waiting for transfers between devices: 53.8 us -> 19.6 us
  starting transfers between devices: 57.7 us -> 26.8 us
  Pallas kernels: 0 us -> 24.4 us
  other arithmetic: 9.01 us -> 1.43 us
  between operations: 6.59 us -> 1.7 us
    psum x3 -> x0, blocking collectives: 93.3 us -> none  [the longest x2 63 us: global_squares(): return lax.psum(jnp.sum(source * source), ('tm', 'lat'))]
    dot_general x189 -> x0, matrix products: 49.5 us -> none  [convolve_padded(): jnp.einsum('oi,ril->rol', kernel[row_off, col_off], window, preferred_ele...]
    ppermute x29 -> x24, waiting for transfers between devices: 53.8 us -> 19.6 us  [the longest x12 11 us: by_partner(): lax.ppermute(value, 'lat', [(i, i ^ shift) for i in range(count)])]
    ppermute x29 -> x24, starting transfers between devices: 57.7 us -> 26.8 us  [the longest x12 19.5 us: by_partner(): lax.ppermute(value, 'lat', [(i, i ^ shift) for i in range(count)])]
    pallas_call x0 -> x11, Pallas kernels: none -> 24.4 us  [the longest x10 22.5 us: call(): pl.pallas_call(kernel, name=name, out_shape=outs, in_specs=specs, out_spe...]
    scatter-add x3 -> x0, other arithmetic: 4.6 us -> none  [observe_adjoint(): tile_table = jnp.zeros((like.size // TILE, TILE), jnp.float32).at[tile_in...]
    unnamed x23 -> x37, local copies, waits for them, and re-layouts: 4.48 us -> 7.38 us
  transfers between devices with their start and end apart: 29 -> 24, of which waited for: 24 -> 8; matrix products, arithmetic and copies ran while one was open for 4% -> 2% of each run, Pallas kernels for 0% -> 18%
where the time goes in v1:
time: 82.2 us; the launch traced here: 82.5 us
  starting transfers between devices  26.8 us (33%)
  Pallas kernels  24.4 us (30%)
  waiting for transfers between devices  19.6 us (24%)
  local copies, waits for them, and re-layouts  8.57 us (10%)
  between operations  1.7 us (2%)
  other arithmetic  1.43 us (2%)
    pallas_call x10, Pallas kernels, call(): pl.pallas_call(kernel, name=name, out_shape=outs, in_specs=specs, out_spe...  22.5 us
    ppermute x12, starting transfers between devices, by_partner(): lax.ppermute(value, 'lat', [(i, i ^ shift) for i in range(count)])  19.5 us
    ppermute x12, waiting for transfers between devices, by_partner(): lax.ppermute(value, 'lat', [(i, i ^ shift) for i in range(count)])  11 us
    unnamed x37, local copies, waits for them, and re-layouts  7.38 us
    ppermute x9, waiting for transfers between devices, along_tm(): lax.ppermute(value, 'tm', [(i, (i + step) % count) for i in range(count)])  5.68 us
    ppermute x9, starting transfers between devices, along_tm(): lax.ppermute(value, 'tm', [(i, (i + step) % count) for i in range(count)])  4.6 us
    ppermute x3, waiting for transfers between devices, row_plan(): lax.ppermute(dots, 'tm', [(i, i ^ step) for i in range(count)])  2.97 us
    ppermute x3, starting transfers between devices, row_plan(): lax.ppermute(dots, 'tm', [(i, i ^ step) for i in range(count)])  2.65 us
  transfers between devices with their start and end apart: 24, of which 8 were waited for; matrix products, arithmetic and copies ran while one was open for 2% of the time, Pallas kernels for 18%

profile of v1, /device:TPU:0, one launch (start us, length us, event | category | flops | bytes accessed | tf_op | source)
XLA Modules:
  0.0 82.5 jit_solution(11594956599409727725)
XLA Ops:
  0.6 1.2 %convert_bitcast_fusion = (bf16[2,69,256]{2,0,1:T(2,128)(2,1)S(1)}, bf16[2,69,256]{2,0,1:T(2,128)(2,1)S(1)}) fusion(f32[1,2,69,256]{3,1,2,0:T(2,128)} %param.12, f32[1,2,69,256]{3,1,2,0:T(2,128)} %param.11), kind=kLoop, calls=%fused_computation.27 | loop fusion | flops 105984 | bytes 423936 | tf_op jit(solution)/shard_map/convert_element_type | solution.py:433
  1.9 3.1 %collective-permute-start = (bf16[144,256]{1,0:T(8,128)(2,1)S(1)}, bf16[144,256]{1,0:T(8,128)(2,1)S(1)}, u32[]{:S(2)}, u32[]{:S(2)}) collective-permute-start(bf16[144,256]{1,0:T(8,128)(2,1)S(1)} %bitcast.50), channel_id=1, source_target_pairs={{0,1},{1,0},{2,3},{3,2},{4,5},{5,4},{6,7},{7,6},{8,9},{9,8},{10,11... | collective-permute-start | bytes 221192 | tf_op jit(solution)/shard_map/ppermute | solution.py:440
  4.9 2.6 %collective-permute-start.1 = (bf16[144,256]{1,0:T(8,128)(2,1)S(1)}, bf16[144,256]{1,0:T(8,128)(2,1)S(1)}, u32[]{:S(2)}, u32[]{:S(2)}) collective-permute-start(bf16[144,256]{1,0:T(8,128)(2,1)S(1)} %bitcast.51), channel_id=1, source_target_pairs={{0,2},{1,3},{2,0},{3,1},{4,6},{5,7},{6,4},{7,5},{8,10},{9,11},{10,... | collective-permute-start | bytes 221192 | tf_op jit(solution)/shard_map/ppermute | solution.py:440
  7.6 1.0 %collective-permute-start.7 = (bf16[144,256]{1,0:T(8,128)(2,1)S(1)}, bf16[144,256]{1,0:T(8,128)(2,1)S(1)}, u32[]{:S(2)}, u32[]{:S(2)}) collective-permute-start(bf16[144,256]{1,0:T(8,128)(2,1)S(1)} %bitcast.64), channel_id=1, source_target_pairs={{0,1},{1,0},{2,3},{3,2},{4,5},{5,4},{6,7},{7,6},{8,9},{9,8},{10,11... | collective-permute-start | bytes 221192 | tf_op jit(solution)/shard_map/ppermute | solution.py:440
  8.5 3.5 %collective-permute-start.8 = (bf16[144,256]{1,0:T(8,128)(2,1)S(1)}, bf16[144,256]{1,0:T(8,128)(2,1)S(1)}, u32[]{:S(2)}, u32[]{:S(2)}) collective-permute-start(bf16[144,256]{1,0:T(8,128)(2,1)S(1)} %bitcast.65), channel_id=1, source_target_pairs={{0,2},{1,3},{2,0},{3,1},{4,6},{5,7},{6,4},{7,5},{8,10},{9,11},{10,... | collective-permute-start | bytes 221192 | tf_op jit(solution)/shard_map/ppermute | solution.py:440
  13.5 0.9 %copy-done.7 = f32[1,256,128]{2,1,0:T(8,128)S(1)} copy-done((f32[1,256,128]{2,1,0:T(8,128)S(1)}, f32[1,256,128]{2,1,0:T(8,128)}, u32[]{:S(2)}) %copy-start.7) | copy-done | bytes 131096
  14.6 0.8 copy-done.4
  18.6 3.9 %collective-permute-start.5 = (bf16[272,128]{1,0:T(8,128)(2,1)S(1)}, bf16[272,128]{1,0:T(8,128)(2,1)S(1)}, u32[]{:S(2)}, u32[]{:S(2)}) collective-permute-start(bf16[272,128]{1,0:T(8,128)(2,1)S(1)} %concatenate.33.o0), channel_id=1, source_target_pairs={{0,2},{1,3},{2,0},{3,1},{4,6},{5,7},{6,4},{7,5},{8,10},{9,11},{10,... | collective-permute-start | bytes 208904 | tf_op jit(solution)/shard_map/ppermute | solution.py:440
  22.6 0.7 gate.1
  23.4 3.2 %collective-permute-done.5.o2 = bf16[272,128]{1,0:T(8,128)(2,1)S(1)} collective-permute-done((bf16[272,128]{1,0:T(8,128)(2,1)S(1)}, bf16[272,128]{1,0:T(8,128)(2,1)S(1)}, u32[]{:S(2)}, u32[]{:S(2)}) %collective-permute-start.5) | collective-permute-done | bytes 69664 | tf_op jit(solution)/shard_map/ppermute | solution.py:440
  26.6 2.1 %collective-permute-done.6.o3 = bf16[272,128]{1,0:T(8,128)(2,1)S(1)} collective-permute-done((bf16[272,128]{1,0:T(8,128)(2,1)S(1)}, bf16[272,128]{1,0:T(8,128)(2,1)S(1)}, u32[]{:S(2)}, u32[]{:S(2)}) %collective-permute-start.6) | collective-permute-done | bytes 69664 | tf_op jit(solution)/shard_map/ppermute | solution.py:440
  28.7 3.7 %rhs.1 = (f32[4,144,256]{2,1,0:T(8,128)S(1)}, bf16[4,144,256]{2,1,0:T(8,128)(2,1)S(1)}) custom-call(s32[1]{0:T(128)S(6)} %copy.44.counts, bf16[144,256]{1,0:T(8,128)(2,1)S(1)} %bitcast.54, bf16[144,256]{1,0:T(8,128)(2,1)S(1)} %collective-permute-done.y1, bf16[144,256]{1,0:T(8,128)(2,1)S(1)} %collective-permute-done.1.y2, ...), custom_call_target="tpu_custom_call" | custom-call | tf_op jit(solution)/shard_map/rhs/pallas_call | solution.py:405
  32.6 3.2 %forward.2 = (f32[4,144,256]{2,1,0:T(8,128)S(1)}, bf16[4,144,256]{2,1,0:T(8,128)(2,1)S(1)}) custom-call(s32[1]{0:T(128)S(6)} %copy.44.counts, f32[4,144,256]{2,1,0:T(8,128)S(1)} %get-tuple-element.14.start.first, bf16[8,128,256]{2,1,0:T(8,128)(2,1)S(1)} %gate.1, bf16[384,240]{1,0:T(8,128)(2,1)S(1)} %reshape.57.w_in, bf16[864,256]{1,0:T(8,128)(2,1)S(1)} %bitcast.48), custom_call_target="tpu_custom_call" | custom-call | tf_op jit(solution)/shard_map/forward/pallas_call | solution.py:405
  36.3 2.4 %collective-permute-start.13 = (bf16[144,256]{1,0:T(8,128)(2,1)S(1)}, bf16[144,256]{1,0:T(8,128)(2,1)S(1)}, u32[]{:S(2)}, u32[]{:S(2)}) collective-permute-start(bf16[144,256]{1,0:T(8,128)(2,1)S(1)} %bitcast.55), channel_id=1, source_target_pairs={{0,1},{1,0},{2,3},{3,2},{4,5},{5,4},{6,7},{7,6},{8,9},{9,8},{10,11... | collective-permute-start | bytes 221192 | tf_op jit(solution)/shard_map/ppermute | solution.py:440
  39.0 2.1 %collective-permute-start.17 = (bf16[144,256]{1,0:T(8,128)(2,1)S(1)}, bf16[144,256]{1,0:T(8,128)(2,1)S(1)}, u32[]{:S(2)}, u32[]{:S(2)}) collective-permute-start(bf16[144,256]{1,0:T(8,128)(2,1)S(1)} %bitcast.57), channel_id=1, source_target_pairs={{0,3},{1,2},{2,1},{3,0},{4,7},{5,6},{6,5},{7,4},{8,11},{9,10},{10,... | collective-permute-start | bytes 221192 | tf_op jit(solution)/shard_map/ppermute | solution.py:440
  41.6 1.1 %collective-permute-start.12 = (bf16[144,256]{1,0:T(8,128)(2,1)S(1)}, bf16[144,256]{1,0:T(8,128)(2,1)S(1)}, u32[]{:S(2)}, u32[]{:S(2)}) collective-permute-start(bf16[144,256]{1,0:T(8,128)(2,1)S(1)} %bitcast.58), channel_id=1, source_target_pairs={{0,12},{4,0},{8,4},{12,8},{1,13},{5,1},{9,5},{13,9},{2,14},{6,2},{... | collective-permute-start | bytes 221192 | tf_op jit(solution)/shard_map/ppermute | solution.py:446
  42.7 5.1 %collective-permute-done.15.p2 = bf16[144,256]{1,0:T(8,128)(2,1)S(1)} collective-permute-done((bf16[144,256]{1,0:T(8,128)(2,1)S(1)}, bf16[144,256]{1,0:T(8,128)(2,1)S(1)}, u32[]{:S(2)}, u32[]{:S(2)}) %collective-permute-start.15) | collective-permute-done | bytes 73760 | tf_op jit(solution)/shard_map/ppermute | solution.py:440
  48.7 2.2 %observe.2.observed = f32[4,144,256]{2,1,0:T(8,128)S(1)} custom-call(f32[4,144,256]{2,1,0:T(8,128)S(1)} %get-tuple-element.16.z, bf16[272,128]{1,0:T(8,128)(2,1)S(1)} %concatenate.33.o0, bf16[272,128]{1,0:T(8,128)(2,1)S(1)} %collective-permute-done.4.o1, bf16[272,128]{1,0:T(8,128)(2,1)S(1)} %collective-permute-done.5.o2, ...), custom_call_target="tpu_custom_call" | custom-call | tf_op jit(solution)/shard_map/observe/pallas_call | solution.py:405
  50.9 0.8 collective-permute-done.18.p3
  51.7 3.3 %adjoint.2 = f32[4,144,256]{2,1,0:T(8,128)S(1)} custom-call(s32[1]{0:T(128)S(6)} %copy.44.counts, f32[4,144,256]{2,1,0:T(8,128)S(1)} %observe.2.observed, f32[4,144,256]{2,1,0:T(8,128)S(1)} %get-tuple-element.16.z, bf16[4,144,256]{2,1,0:T(8,128)(2,1)S(1)} %collective-permute-done.11.later, bf16[144,256]{1,0:T(8,128)(2,1)S(1)} %collective-permute-done.12.p0, ...), custom_call_target="tpu_custom_call" | custom-call | tf_op jit(solution)/shard_map/adjoint/pallas_call | solution.py:405
  55.2 3.2 %forward.3 = (f32[4,144,256]{2,1,0:T(8,128)S(1)}, bf16[4,144,256]{2,1,0:T(8,128)(2,1)S(1)}) custom-call(s32[1]{0:T(128)S(6)} %copy.44.counts, f32[4,144,256]{2,1,0:T(8,128)S(1)} %get-tuple-element.18.start.second, bf16[8,128,256]{2,1,0:T(8,128)(2,1)S(1)} %gate.1, bf16[384,240]{1,0:T(8,128)(2,1)S(1)} %reshape.57.w_in, bf16[864,256]{1,0:T(8,128)(2,1)S(1)} %bitcast.49), custom_call_target="tpu_custom_call" | custom-call | tf_op jit(solution)/shard_map/forward/pallas_call | solution.py:405
  58.4 2.0 %collective-permute-start.20 = (bf16[4,144,256]{2,1,0:T(8,128)(2,1)S(1)}, bf16[4,144,256]{2,1,0:T(8,128)(2,1)S(1)}, u32[]{:S(2)}, u32[]{:S(2)}) collective-permute-start(bf16[4,144,256]{2,1,0:T(8,128)(2,1)S(1)} %get-tuple-element.21), channel_id=1, source_target_pairs={{0,12},{4,0},{8,4},{12,8},{1,13},{5,1},{9,5},{13,9},{2,14},{6,2},{... | collective-permute-start | bytes 884744 | tf_op jit(solution)/shard_map/ppermute | solution.py:446
  60.4 2.2 %observe.3.observed = f32[4,144,256]{2,1,0:T(8,128)S(1)} custom-call(f32[4,144,256]{2,1,0:T(8,128)S(1)} %get-tuple-element.20.z, bf16[272,128]{1,0:T(8,128)(2,1)S(1)} %concatenate.33.o0, bf16[272,128]{1,0:T(8,128)(2,1)S(1)} %collective-permute-done.4.o1, bf16[272,128]{1,0:T(8,128)(2,1)S(1)} %collective-permute-done.5.o2, ...), custom_call_target="tpu_custom_call" | custom-call | tf_op jit(solution)/shard_map/observe/pallas_call | solution.py:405
  62.6 4.9 %collective-permute-done.20.later = bf16[4,144,256]{2,1,0:T(8,128)(2,1)S(1)} collective-permute-done((bf16[4,144,256]{2,1,0:T(8,128)(2,1)S(1)}, bf16[4,144,256]{2,1,0:T(8,128)(2,1)S(1)}, u32[]{:S(2)}, u32[]{:S(2)}) %collective-permute-start.20) | collective-permute-done | bytes 294944 | tf_op jit(solution)/shard_map/ppermute | solution.py:446
  67.5 3.3 %adjoint.3 = f32[4,144,256]{2,1,0:T(8,128)S(1)} custom-call(s32[1]{0:T(128)S(6)} %copy.44.counts, f32[4,144,256]{2,1,0:T(8,128)S(1)} %observe.3.observed, f32[4,144,256]{2,1,0:T(8,128)S(1)} %get-tuple-element.20.z, bf16[4,144,256]{2,1,0:T(8,128)(2,1)S(1)} %collective-permute-done.20.later, bf16[144,256]{1,0:T(8,128)(2,1)S(1)} %collective-permute-done.12.p0, ...), custom_call_target="tpu_custom_call" | custom-call | tf_op jit(solution)/shard_map/adjoint/pallas_call | solution.py:405
  71.9 1.3 %collective-permute-start.21 = (f32[8,128]{1,0:T(8,128)S(1)}, f32[8,128]{1,0:T(8,128)S(1)}, u32[]{:S(2)}, u32[]{:S(2)}) collective-permute-start(f32[8,128]{1,0:T(8,128)S(1)} %get-tuple-element.22.d0), channel_id=1, source_target_pairs={{0,4},{4,0},{8,12},{12,8},{1,5},{5,1},{9,13},{13,9},{2,6},{6,2},{1... | collective-permute-start | bytes 12296 | tf_op jit(solution)/shard_map/ppermute | solution.py:548
  73.2 1.3 %collective-permute-start.22 = (f32[8,128]{1,0:T(8,128)S(1)}, f32[8,128]{1,0:T(8,128)S(1)}, u32[]{:S(2)}, u32[]{:S(2)}) collective-permute-start(f32[8,128]{1,0:T(8,128)S(1)} %get-tuple-element.22.d0), channel_id=1, source_target_pairs={{0,8},{4,12},{8,0},{12,4},{1,9},{5,13},{9,1},{13,5},{2,10},{6,14},... | collective-permute-start | bytes 12296 | tf_op jit(solution)/shard_map/ppermute | solution.py:548
  74.6 2.2 %collective-permute-done.22.d2 = f32[8,128]{1,0:T(8,128)S(1)} collective-permute-done((f32[8,128]{1,0:T(8,128)S(1)}, f32[8,128]{1,0:T(8,128)S(1)}, u32[]{:S(2)}, u32[]{:S(2)}) %collective-permute-start.22) | collective-permute-done | bytes 4128 | tf_op jit(solution)/shard_map/ppermute | solution.py:548
  76.8 0.7 collective-permute-done.23.d3
  78.2 1.9 %finish.1 = (f32[2,69,256]{2,1,0:T(8,128)}, f32[2,69,256]{2,1,0:T(8,128)}) custom-call(s32[1]{0:T(128)} %bitcast.lat_at, f32[8,128]{1,0:T(8,128)} %copy-done.3, f32[8,128]{1,0:T(8,128)} %copy-done.9, f32[8,128]{1,0:T(8,128)} %copy-done.10, f32[8,128]{1,0:T(8,128)} %copy-done.11, f32[4,144,256]{2,1,0:T(8,128)} %copy-done, f32[4,144,256]{2,1,0:T(8,128)} %copy-done.1, ...), custom_call_target="tpu_custom_call" | custom-call | tf_op jit(solution)/shard_map/finish/pallas_call | solution.py:554
  80.1 1.7 %copy.35 = f32[1,2,69,256]{3,1,2,0:T(2,128)} copy(f32[1,2,69,256]{3,2,1,0:T(8,128)} %bitcast.69) | data formatting | bytes 282624
  81.7 0.7 copy.36
  (89 shorter events, 8.7 us)
Async XLA Ops:
  1.8 5.7 %copy-start.8 = (bf16[1,2,69,256]{3,1,2,0:T(2,128)(2,1)S(1)}, bf16[1,2,69,256]{3,1,2,0:T(2,128)(2,1)}, u32[]{:S(2)}) copy-start(bf16[1,2,69,256]{3,1,2,0:T(2,128)(2,1)} %param.13) | copy-start | bytes 211972
  1.8 10.2 %copy-start.5 = (bf16[3,3,128,69]{2,3,1,0:T(8,128)(2,1)S(1)}, bf16[3,3,128,69]{2,3,1,0:T(8,128)(2,1)}, u32[]{:S(2)}) copy-start(bf16[3,3,128,69]{2,3,1,0:T(8,128)(2,1)} %param.14) | copy-start | bytes 476932
  1.9 13.6 %collective-permute-start = (bf16[144,256]{1,0:T(8,128)(2,1)S(1)}, bf16[144,256]{1,0:T(8,128)(2,1)S(1)}, u32[]{:S(2)}, u32[]{:S(2)}) collective-permute-start(bf16[144,256]{1,0:T(8,128)(2,1)S(1)} %bitcast.50), channel_id=1, source_target_pairs={{0,1},{1,0},{2,3},{3,2},{4,5},{5,4},{6,7},{7,6},{8,9},{9,8},{10,11... | collective-permute-start | bytes 221192 | tf_op jit(solution)/shard_map/ppermute | solution.py:440
  4.9 10.6 %collective-permute-start.1 = (bf16[144,256]{1,0:T(8,128)(2,1)S(1)}, bf16[144,256]{1,0:T(8,128)(2,1)S(1)}, u32[]{:S(2)}, u32[]{:S(2)}) collective-permute-start(bf16[144,256]{1,0:T(8,128)(2,1)S(1)} %bitcast.51), channel_id=1, source_target_pairs={{0,2},{1,3},{2,0},{3,1},{4,6},{5,7},{6,4},{7,5},{8,10},{9,11},{10,... | collective-permute-start | bytes 221192 | tf_op jit(solution)/shard_map/ppermute | solution.py:440
  7.5 8.5 %collective-permute-start.2 = (bf16[144,256]{1,0:T(8,128)(2,1)S(1)}, bf16[144,256]{1,0:T(8,128)(2,1)S(1)}, u32[]{:S(2)}, u32[]{:S(2)}) collective-permute-start(bf16[144,256]{1,0:T(8,128)(2,1)S(1)} %bitcast.52), channel_id=1, source_target_pairs={{0,3},{1,2},{2,1},{3,0},{4,7},{5,6},{6,5},{7,4},{8,11},{9,10},{10,... | collective-permute-start | bytes 221192 | tf_op jit(solution)/shard_map/ppermute | solution.py:440
  7.6 11.0 %collective-permute-start.7 = (bf16[144,256]{1,0:T(8,128)(2,1)S(1)}, bf16[144,256]{1,0:T(8,128)(2,1)S(1)}, u32[]{:S(2)}, u32[]{:S(2)}) collective-permute-start(bf16[144,256]{1,0:T(8,128)(2,1)S(1)} %bitcast.64), channel_id=1, source_target_pairs={{0,1},{1,0},{2,3},{3,2},{4,5},{5,4},{6,7},{7,6},{8,9},{9,8},{10,11... | collective-permute-start | bytes 221192 | tf_op jit(solution)/shard_map/ppermute | solution.py:440
  8.5 14.0 %collective-permute-start.8 = (bf16[144,256]{1,0:T(8,128)(2,1)S(1)}, bf16[144,256]{1,0:T(8,128)(2,1)S(1)}, u32[]{:S(2)}, u32[]{:S(2)}) collective-permute-start(bf16[144,256]{1,0:T(8,128)(2,1)S(1)} %bitcast.65), channel_id=1, source_target_pairs={{0,2},{1,3},{2,0},{3,1},{4,6},{5,7},{6,4},{7,5},{8,10},{9,11},{10,... | collective-permute-start | bytes 221192 | tf_op jit(solution)/shard_map/ppermute | solution.py:440
  14.5 0.9 %copy-start.4 = (bf16[3,3,69,128]{3,2,1,0:T(8,128)(2,1)S(1)}, bf16[3,3,69,128]{3,2,1,0:T(8,128)(2,1)}, u32[]{:S(2)}) copy-start(bf16[3,3,69,128]{3,2,1,0:T(8,128)(2,1)} %param.15) | copy-start | bytes 476932
  15.4 7.2 %collective-permute-start.9 = (bf16[144,256]{1,0:T(8,128)(2,1)S(1)}, bf16[144,256]{1,0:T(8,128)(2,1)S(1)}, u32[]{:S(2)}, u32[]{:S(2)}) collective-permute-start(bf16[144,256]{1,0:T(8,128)(2,1)S(1)} %bitcast.66), channel_id=1, source_target_pairs={{0,3},{1,2},{2,1},{3,0},{4,7},{5,6},{6,5},{7,4},{8,11},{9,10},{10,... | collective-permute-start | bytes 221192 | tf_op jit(solution)/shard_map/ppermute | solution.py:440
  15.5 7.8 %collective-permute-start.4 = (bf16[272,128]{1,0:T(8,128)(2,1)S(1)}, bf16[272,128]{1,0:T(8,128)(2,1)S(1)}, u32[]{:S(2)}, u32[]{:S(2)}) collective-permute-start(bf16[272,128]{1,0:T(8,128)(2,1)S(1)} %concatenate.33.o0), channel_id=1, source_target_pairs={{0,1},{1,0},{2,3},{3,2},{4,5},{5,4},{6,7},{7,6},{8,9},{9,8},{10,11... | collective-permute-start | bytes 208904 | tf_op jit(solution)/shard_map/ppermute | solution.py:440
  16.1 12.6 %collective-permute-start.3 = (bf16[4,144,256]{2,1,0:T(8,128)(2,1)S(1)}, bf16[4,144,256]{2,1,0:T(8,128)(2,1)S(1)}, u32[]{:S(2)}, u32[]{:S(2)}) collective-permute-start(bf16[4,144,256]{2,1,0:T(8,128)(2,1)S(1)} %pad_maximum_fusion), channel_id=1, source_target_pairs={{0,12},{4,0},{8,4},{12,8},{1,13},{5,1},{9,5},{13,9},{2,14},{6,2},{... | collective-permute-start | bytes 884744 | tf_op jit(solution)/shard_map/ppermute | solution.py:446
  18.6 8.0 %collective-permute-start.5 = (bf16[272,128]{1,0:T(8,128)(2,1)S(1)}, bf16[272,128]{1,0:T(8,128)(2,1)S(1)}, u32[]{:S(2)}, u32[]{:S(2)}) collective-permute-start(bf16[272,128]{1,0:T(8,128)(2,1)S(1)} %concatenate.33.o0), channel_id=1, source_target_pairs={{0,2},{1,3},{2,0},{3,1},{4,6},{5,7},{6,4},{7,5},{8,10},{9,11},{10,... | collective-permute-start | bytes 208904 | tf_op jit(solution)/shard_map/ppermute | solution.py:440
  22.5 6.2 %collective-permute-start.6 = (bf16[272,128]{1,0:T(8,128)(2,1)S(1)}, bf16[272,128]{1,0:T(8,128)(2,1)S(1)}, u32[]{:S(2)}, u32[]{:S(2)}) collective-permute-start(bf16[272,128]{1,0:T(8,128)(2,1)S(1)} %concatenate.33.o0), channel_id=1, source_target_pairs={{0,3},{1,2},{2,1},{3,0},{4,7},{5,6},{6,5},{7,4},{8,11},{9,10},{10,... | collective-permute-start | bytes 208904 | tf_op jit(solution)/shard_map/ppermute | solution.py:440
  32.4 38.4 %copy-start = (f32[4,144,256]{2,1,0:T(8,128)}, f32[4,144,256]{2,1,0:T(8,128)S(1)}, u32[]{:S(2)}) copy-start(f32[4,144,256]{2,1,0:T(8,128)S(1)} %get-tuple-element.14.start.first) | copy-start | bytes 1769476
  32.4 19.3 %collective-permute-start.11 = (bf16[4,144,256]{2,1,0:T(8,128)(2,1)S(1)}, bf16[4,144,256]{2,1,0:T(8,128)(2,1)S(1)}, u32[]{:S(2)}, u32[]{:S(2)}) collective-permute-start(bf16[4,144,256]{2,1,0:T(8,128)(2,1)S(1)} %get-tuple-element.17), channel_id=1, source_target_pairs={{0,12},{4,0},{8,4},{12,8},{1,13},{5,1},{9,5},{13,9},{2,14},{6,2},{... | collective-permute-start | bytes 884744 | tf_op jit(solution)/shard_map/ppermute | solution.py:446
  35.8 19.2 %collective-permute-start.10 = (bf16[4,144,256]{2,1,0:T(8,128)(2,1)S(1)}, bf16[4,144,256]{2,1,0:T(8,128)(2,1)S(1)}, u32[]{:S(2)}, u32[]{:S(2)}) collective-permute-start(bf16[4,144,256]{2,1,0:T(8,128)(2,1)S(1)} %get-tuple-element.15), channel_id=1, source_target_pairs={{0,4},{4,8},{8,12},{12,0},{1,5},{5,9},{9,13},{13,1},{2,6},{6,10},{... | collective-permute-start | bytes 884744 | tf_op jit(solution)/shard_map/ppermute | solution.py:446
  36.3 5.4 %collective-permute-start.13 = (bf16[144,256]{1,0:T(8,128)(2,1)S(1)}, bf16[144,256]{1,0:T(8,128)(2,1)S(1)}, u32[]{:S(2)}, u32[]{:S(2)}) collective-permute-start(bf16[144,256]{1,0:T(8,128)(2,1)S(1)} %bitcast.55), channel_id=1, source_target_pairs={{0,1},{1,0},{2,3},{3,2},{4,5},{5,4},{6,7},{7,6},{8,9},{9,8},{10,11... | collective-permute-start | bytes 221192 | tf_op jit(solution)/shard_map/ppermute | solution.py:440
  38.6 9.2 %collective-permute-start.15 = (bf16[144,256]{1,0:T(8,128)(2,1)S(1)}, bf16[144,256]{1,0:T(8,128)(2,1)S(1)}, u32[]{:S(2)}, u32[]{:S(2)}) collective-permute-start(bf16[144,256]{1,0:T(8,128)(2,1)S(1)} %bitcast.56), channel_id=1, source_target_pairs={{0,2},{1,3},{2,0},{3,1},{4,6},{5,7},{6,4},{7,5},{8,10},{9,11},{10,... | collective-permute-start | bytes 221192 | tf_op jit(solution)/shard_map/ppermute | solution.py:440
  39.0 9.2 %collective-permute-start.17 = (bf16[144,256]{1,0:T(8,128)(2,1)S(1)}, bf16[144,256]{1,0:T(8,128)(2,1)S(1)}, u32[]{:S(2)}, u32[]{:S(2)}) collective-permute-start(bf16[144,256]{1,0:T(8,128)(2,1)S(1)} %bitcast.57), channel_id=1, source_target_pairs={{0,3},{1,2},{2,1},{3,0},{4,7},{5,6},{6,5},{7,4},{8,11},{9,10},{10,... | collective-permute-start | bytes 221192 | tf_op jit(solution)/shard_map/ppermute | solution.py:440
  41.6 7.0 %collective-permute-start.12 = (bf16[144,256]{1,0:T(8,128)(2,1)S(1)}, bf16[144,256]{1,0:T(8,128)(2,1)S(1)}, u32[]{:S(2)}, u32[]{:S(2)}) collective-permute-start(bf16[144,256]{1,0:T(8,128)(2,1)S(1)} %bitcast.58), channel_id=1, source_target_pairs={{0,12},{4,0},{8,4},{12,8},{1,13},{5,1},{9,5},{13,9},{2,14},{6,2},{... | collective-permute-start | bytes 221192 | tf_op jit(solution)/shard_map/ppermute | solution.py:446
  47.8 3.1 %collective-permute-start.14 = (bf16[144,256]{1,0:T(8,128)(2,1)S(1)}, bf16[144,256]{1,0:T(8,128)(2,1)S(1)}, u32[]{:S(2)}, u32[]{:S(2)}) collective-permute-start(bf16[144,256]{1,0:T(8,128)(2,1)S(1)} %collective-permute-done.13.p1), channel_id=1, source_target_pairs={{0,12},{4,0},{8,4},{12,8},{1,13},{5,1},{9,5},{13,9},{2,14},{6,2},{... | collective-permute-start | bytes 221192 | tf_op jit(solution)/shard_map/ppermute | solution.py:446
  48.2 2.7 %collective-permute-start.16 = (bf16[144,256]{1,0:T(8,128)(2,1)S(1)}, bf16[144,256]{1,0:T(8,128)(2,1)S(1)}, u32[]{:S(2)}, u32[]{:S(2)}) collective-permute-start(bf16[144,256]{1,0:T(8,128)(2,1)S(1)} %collective-permute-done.15.p2), channel_id=1, source_target_pairs={{0,12},{4,0},{8,4},{12,8},{1,13},{5,1},{9,5},{13,9},{2,14},{6,2},{... | collective-permute-start | bytes 221192 | tf_op jit(solution)/shard_map/ppermute | solution.py:446
  48.6 3.0 %collective-permute-start.18 = (bf16[144,256]{1,0:T(8,128)(2,1)S(1)}, bf16[144,256]{1,0:T(8,128)(2,1)S(1)}, u32[]{:S(2)}, u32[]{:S(2)}) collective-permute-start(bf16[144,256]{1,0:T(8,128)(2,1)S(1)} %collective-permute-done.17.p3), channel_id=1, source_target_pairs={{0,12},{4,0},{8,4},{12,8},{1,13},{5,1},{9,5},{13,9},{2,14},{6,2},{... | collective-permute-start | bytes 221192 | tf_op jit(solution)/shard_map/ppermute | solution.py:446
  55.2 15.6 %copy-start.1 = (f32[4,144,256]{2,1,0:T(8,128)}, f32[4,144,256]{2,1,0:T(8,128)S(1)}, u32[]{:S(2)}) copy-start(f32[4,144,256]{2,1,0:T(8,128)S(1)} %get-tuple-element.18.start.second) | copy-start | bytes 1769476
  58.4 9.0 %collective-permute-start.20 = (bf16[4,144,256]{2,1,0:T(8,128)(2,1)S(1)}, bf16[4,144,256]{2,1,0:T(8,128)(2,1)S(1)}, u32[]{:S(2)}, u32[]{:S(2)}) collective-permute-start(bf16[4,144,256]{2,1,0:T(8,128)(2,1)S(1)} %get-tuple-element.21), channel_id=1, source_target_pairs={{0,12},{4,0},{8,4},{12,8},{1,13},{5,1},{9,5},{13,9},{2,14},{6,2},{... | collective-permute-start | bytes 884744 | tf_op jit(solution)/shard_map/ppermute | solution.py:446
  60.4 10.4 %collective-permute-start.19 = (bf16[4,144,256]{2,1,0:T(8,128)(2,1)S(1)}, bf16[4,144,256]{2,1,0:T(8,128)(2,1)S(1)}, u32[]{:S(2)}, u32[]{:S(2)}) collective-permute-start(bf16[4,144,256]{2,1,0:T(8,128)(2,1)S(1)} %get-tuple-element.19), channel_id=1, source_target_pairs={{0,4},{4,8},{8,12},{12,0},{1,5},{5,9},{9,13},{13,1},{2,6},{6,10},{... | collective-permute-start | bytes 884744 | tf_op jit(solution)/shard_map/ppermute | solution.py:446
  71.9 5.6 %copy-start.3 = (f32[8,128]{1,0:T(8,128)}, f32[8,128]{1,0:T(8,128)S(1)}, u32[]{:S(2)}) copy-start(f32[8,128]{1,0:T(8,128)S(1)} %get-tuple-element.22.d0) | copy-start | bytes 12292
  71.9 2.7 %collective-permute-start.21 = (f32[8,128]{1,0:T(8,128)S(1)}, f32[8,128]{1,0:T(8,128)S(1)}, u32[]{:S(2)}, u32[]{:S(2)}) collective-permute-start(f32[8,128]{1,0:T(8,128)S(1)} %get-tuple-element.22.d0), channel_id=1, source_target_pairs={{0,4},{4,0},{8,12},{12,8},{1,5},{5,1},{9,13},{13,9},{2,6},{6,2},{1... | collective-permute-start | bytes 12296 | tf_op jit(solution)/shard_map/ppermute | solution.py:548
  73.2 3.6 %collective-permute-start.22 = (f32[8,128]{1,0:T(8,128)S(1)}, f32[8,128]{1,0:T(8,128)S(1)}, u32[]{:S(2)}, u32[]{:S(2)}) collective-permute-start(f32[8,128]{1,0:T(8,128)S(1)} %get-tuple-element.22.d0), channel_id=1, source_target_pairs={{0,8},{4,12},{8,0},{12,4},{1,9},{5,13},{9,1},{13,5},{2,10},{6,14},... | collective-permute-start | bytes 12296 | tf_op jit(solution)/shard_map/ppermute | solution.py:548
  74.5 3.0 %collective-permute-start.23 = (f32[8,128]{1,0:T(8,128)S(1)}, f32[8,128]{1,0:T(8,128)S(1)}, u32[]{:S(2)}, u32[]{:S(2)}) collective-permute-start(f32[8,128]{1,0:T(8,128)S(1)} %get-tuple-element.22.d0), channel_id=1, source_target_pairs={{0,12},{4,8},{8,4},{12,0},{1,13},{5,9},{9,5},{13,1},{2,14},{6,10},... | collective-permute-start | bytes 12296 | tf_op jit(solution)/shard_map/ppermute | solution.py:548
  74.6 3.0 %copy-start.9 = (f32[8,128]{1,0:T(8,128)}, f32[8,128]{1,0:T(8,128)S(1)}, u32[]{:S(2)}) copy-start(f32[8,128]{1,0:T(8,128)S(1)} %collective-permute-done.21.d1) | copy-start | bytes 12292
  80.1 1.7 %copy-start.6 = (f32[2,69,256]{2,1,0:T(8,128)S(1)}, f32[2,69,256]{2,1,0:T(8,128)}, u32[]{:S(2)}) copy-start(f32[2,69,256]{2,1,0:T(8,128)} %get-tuple-element.25) | copy-start | bytes 423940
  (8 other events, 5.6 us)
